TPU v7x, 256 devices: a whole 4x4x8 slice. The times are simulated.
256 devices in a mesh: ctx: 8 (over z_hi, y), tp: 32 (over z_lo, x, core).
Axes of the slice: x: 4, y: 4, z: 8 (z_hi: 2, z_lo: 4; z = z_hi * 4 + z_lo), core: 2. Of those that a mesh axis runs over, the one named last changes fastest.
Arguments:
- streams: bfloat16 [3, 1, 3072, 8192], P(None, None, 'ctx', 'tp'), may hold values from -6 to 6
- taps: float32 [3, 7, 8192], P(None, None, 'tp'), may hold values from -2.4 to 2.4
- decay: float32 [16, 8192], P(None, 'tp'), may hold values from 0.96 to 1, as said below
- residues: float32 [16, 8192], P(None, 'tp'), may hold values from -0.12 to 0.12
- init_state: float32 [1, 16, 8192], P(None, None, 'tp'), may hold values from -48 to 48
- out_weight: bfloat16 [8192, 8192], P('tp'), may hold values from -0.125 to 0.125
Outputs:
- mixed: bfloat16 [1, 3072, 8192], P(None, 'ctx', 'tp')
Inputs may be any that keep to these rules, and one draw needn't show every extreme that they name: `decay`: each pole's factor lies strictly between 0 and 1.
All inputs are finite; a program needn't handle non-finite values.
Results may differ from a plain program's by a relative error of at most 0.0049.
Values may be sent and summed in bfloat16 or wider, within the bound.
A program may use at most 128 MiB of HBM per device.

v0:
```python
import jax
import jax.numpy as jnp
from jax import lax
from jax.sharding import PartitionSpec as P


def passed_along(x, axis, by):
    peers = lax.axis_size(axis)
    pairs = [(i, i + by) for i in range(peers) if 0 <= i + by < peers]
    return lax.ppermute(x, axis, pairs)


def prefix(value, axis, join, neutral):
    count, mine = (lax.axis_size(axis), lax.axis_index(axis))
    pieces = jax.tree.map(lambda part: lax.all_gather(part, axis), value)
    total = jax.tree.map(
        lambda part, zero: jnp.full_like(part, 0) + jnp.asarray(zero, part.dtype), value, neutral
    )

    def step(position, total):
        longer = join(total, jax.tree.map(lambda part: part[position], pieces))
        return jax.tree.map(lambda new, old: jnp.where(position < mine, new, old), longer, total)

    return lax.fori_loop(0, count - 1, step, total)


def per_device(streams, taps, decay, residues, init_state, out_weight):
    highest = lax.Precision.HIGHEST
    tap_count = taps.shape[1]
    tap_lag = tap_count - 1
    length = streams.shape[2]
    rim_rows = passed_along(streams[:, :, length - tap_lag :, :], "ctx", 1)
    joined = jnp.concatenate([rim_rows, streams], axis=2).astype(jnp.float32)
    featured = jnp.zeros(streams.shape, jnp.float32)
    for tap_index in range(tap_count):
        featured = (
            featured
            + taps[:, tap_index][:, None, None, :]
            * joined[:, :, tap_lag - tap_index : tap_lag - tap_index + length, :]
        )
    queries = featured[0]
    driven = featured[1] * featured[2]
    seq_count = driven.shape[0]
    channels = driven.shape[2]
    block_len = min(128, length)
    block_count = length // block_len
    log_decay = jnp.log(decay)
    positions = jnp.arange(block_len).astype(jnp.float32)
    powers = jnp.exp(positions[:, None, None] * log_decay[None])
    kernel = jnp.einsum("tnc,nc->tc", powers, residues, precision=highest)
    offset = jnp.arange(block_len)[:, None] - jnp.arange(block_len)[None, :]
    toeplitz = jnp.where(
        (offset >= 0)[:, :, None], kernel[jnp.maximum(offset, 0)], jnp.float32(0.0)
    )
    blocked = driven.reshape(seq_count, block_count, block_len, channels)
    within = jnp.einsum("tjc,sbjc->sbtc", toeplitz, blocked, precision=highest)
    tail_pow = jnp.exp((block_len - 1 - positions)[:, None, None] * log_decay[None])
    block_end = jnp.einsum("sbjc,jnc->sbnc", blocked, tail_pow, precision=highest)
    block_decay = jnp.exp(block_len * log_decay)

    def advance(running, block_state):
        return (block_decay[None] * running + block_state, running)

    end_local, entry_local = lax.scan(
        advance, jnp.zeros(init_state.shape, jnp.float32), jnp.moveaxis(block_end, 1, 0)
    )
    shard_decay = jnp.exp(length * log_decay)

    def chain_join(earlier, later_part):
        return (earlier[0] * later_part[0], later_part[0][None] * earlier[1] + later_part[1])

    prefix_decay, prefix_state = prefix(
        (shard_decay, end_local),
        "ctx",
        chain_join,
        (jnp.ones_like(shard_decay), jnp.zeros_like(end_local)),
    )
    incoming = prefix_decay[None] * init_state + prefix_state
    block_starts = jnp.exp(
        (block_len * jnp.arange(block_count).astype(jnp.float32))[:, None, None] * log_decay[None]
    )
    entries = entry_local + block_starts[:, None] * incoming[None]
    lead_pow = jnp.exp((positions + 1.0)[:, None, None] * log_decay[None]) * residues[None]
    carried = jnp.einsum("bsnc,tnc->sbtc", entries, lead_pow, precision=highest)
    response = (within + carried).reshape(seq_count, length, channels)
    gated_out = (queries * response).astype(jnp.bfloat16)
    gated_rows = gated_out.reshape(seq_count * length, channels)
    mixed = lax.psum_scatter(
        lax.dot_general(
            out_weight, gated_rows, (((0,), (1,)), ((), ())), preferred_element_type=jnp.float32
        ),
        "tp",
        scatter_dimension=0,
        tiled=True,
    ).T
    return mixed.astype(jnp.bfloat16).reshape(seq_count, length, channels)


def solution(mesh):
    in_specs = (
        P(None, None, "ctx", "tp"),
        P(None, None, "tp"),
        P(None, "tp"),
        P(None, "tp"),
        P(None, None, "tp"),
        P("tp", None),
    )
    out_specs = P(None, "ctx", "tp")
    return jax.shard_map(
        per_device, mesh=mesh, in_specs=in_specs, out_specs=out_specs, check_vma=False
    )
```

profile of v0, /device:TPU:16, one launch (start us, length us, event | category | flops | bytes accessed | tf_op | source)
XLA Modules:
  0.0 407.5 jit_solution(10679517465900434798)
XLA Ops:
  6.5 0.0 copy-start.1
  6.5 0.0 reduce-scatter.2.cloned.1.call-start
  6.5 0.7 slice.55
  7.3 3.2 collective-permute-start
  10.5 1.0 fusion.40
  11.6 0.7 multiply_exponential_fusion
  12.3 0.1 copy.23
  12.4 0.8 copy.45
  13.3 1.7 multiply_reduce_fusion
  14.9 44.2 %all-gather = f32[128,256]{1,0:T(8,128)S(1)} all-gather(f32[16,256]{1,0:T(8,128)S(1)} %get-tuple-element.236), channel_id=2, replica_groups=mesh['ctx'=8,'tp'=32] {'ctx'}, dimensions={0}, use_global_device_ids=true | all-gather | bytes 147456 | tf_op jit(solution)/shard_map/all_gather | solution.py:15
  59.1 0.0 copy-done.1
  59.2 0.1 copy.26
  59.3 0.1 copy.37
  59.4 62.0 %gather_fusion = f32[16384,256]{1,0:T(8,128)} fusion(f32[128,256]{1,0:T(8,128)S(1)} %bitcast.94, s32[16384]{0:T(1024)S(1)} %bitcast_clamp_fusion), kind=kCustom, calls=%fused_computation | custom fusion | bytes 33619968 | tf_op jit(solution)/shard_map/gather | solution.py:53
  121.4 0.0 copy-start
  121.4 18.1 %copy.24 = f32[128,128,256]{1,0,2:T(8,128)} copy(f32[128,128,256]{2,1,0:T(8,128)} %bitcast.95) | data formatting | bytes 33554432 | tf_op jit(solution)/shard_map/gather | solution.py:53
  139.6 0.0 collective-permute-done
  139.6 0.0 copy-done
  139.6 0.1 maximum_convert_fusion
  139.7 1.0 fusion.24
  140.7 0.1 slice_multiply_fusion.7
  140.7 0.2 copy.25
  140.9 3.5 fusion.18
  144.5 0.0 copy-start.2
  144.5 0.1 copy.28
  144.6 0.1 while.29
  144.8 44.0 %all-gather.1 = f32[8,16,256]{2,1,0:T(8,128)S(1)} all-gather(f32[1,16,256]{2,1,0:T(8,128)S(1)} %get-tuple-element.144), channel_id=3, replica_groups=mesh['ctx'=8,'tp'=32] {'ctx'}, dimensions={0}, use_global_device_ids=true | all-gather | bytes 147456 | tf_op jit(solution)/shard_map/all_gather | solution.py:15
  188.8 0.4 while.30
  189.2 0.0 copy-done.2
  189.2 0.1 add_bitcast_fusion
  189.3 0.2 copy.30
  189.5 3.1 fusion.15
  192.6 28.6 %fusion.21 = f32[1,3,128,256]{2,1,3,0:T(4,128)S(1)} fusion(f32[1,3,128,256]{2,1,3,0:T(4,128)S(1)} %fusion.15, f32[3,128,256]{1,0,2:T(4,128)S(1)} %copy.25, f32[128,128,256]{1,0,2:T(8,128)} %copy.24, pred[128,128]{1,0:T(8,128)(4,1)S(1)} %subtract_compare_fusion), kind=kOutput, calls=%fused_computation.23 | convolution fusion | flops 155287552 | bytes 17973248 | tf_op jit(solution)/shard_map/tjc,sbjc->sbtc/dot_general | solution.py:56
  221.2 0.2 copy.31
  221.4 0.1 fusion.36
  221.5 8.5 %convolution_bitcast_fusion = f32[8192,384]{0,1:T(8,128)} fusion(bf16[384,256]{1,0:T(8,128)(2,1)S(1)} %fusion.36, bf16[256,8192]{1,0:T(8,128)(2,1)} %param.15), kind=kOutput, calls=%fused_computation.9 | convolution fusion | flops 1610612736 | bytes 16973824 | tf_op jit(solution)/shard_map/dot_general | solution.py:89
  230.0 0.0 reduce-scatter.2.cloned.1.call-update
  230.0 168.9 %reduce-scatter.2.cloned.1.call-done = f32[256,384]{0,1:T(8,128)} async-done(((f32[8192,384]{0,1:T(8,128)}), f32[256,384]{0,1:T(8,128)}) %reduce-scatter.2.cloned.1.call-update) | async-done | bytes 393232 | tf_op jit(solution)/shard_map/reduce_scatter | solution.py:88
  399.0 1.7 convert_bitcast_fusion
  (35 shorter events, 0.3 us)
Async XLA Ops:
  6.5 52.6 %copy-start.1 = (f32[16,256]{1,0:T(8,128)S(1)}, f32[16,256]{1,0:T(8,128)}, u32[]{:S(2)}) copy-start(f32[16,256]{1,0:T(8,128)} %param.13) | copy-start | bytes 49156
  6.5 392.4 %reduce-scatter.2.cloned.1.call-start = ((), (), s32[]{:S(2)}) async-start(), calls=%async_computation.1 | async-start | bytes 12976128 | tf_op jit(solution)/shard_map/reduce_scatter | solution.py:88
  7.3 132.3 %collective-permute-start = (bf16[3,1,6,256]{3,2,1,0:T(8,128)(2,1)S(1)}, bf16[3,1,6,256]{3,2,1,0:T(8,128)(2,1)S(1)}, u32[]{:S(2)}, u32[]{:S(2)}) collective-permute-start(bf16[3,1,6,256]{3,2,1,0:T(8,128)(2,1)S(1)} %slice.55), channel_id=1, source_target_pairs={{0,32},{32,64},{64,96},{96,128},{128,160},{160,192},{192,224},{1,3... | collective-permute-start | bytes 27656 | tf_op jit(solution)/shard_map/ppermute | solution.py:10
  121.4 18.2 %copy-start = (bf16[3,1,384,256]{3,2,1,0:T(8,128)(2,1)S(1)}, bf16[3,1,384,256]{3,2,1,0:T(8,128)(2,1)}, u32[]{:S(2)}) copy-start(bf16[3,1,384,256]{3,2,1,0:T(8,128)(2,1)} %param.10) | copy-start | bytes 1769476
  144.5 44.7 %copy-start.2 = (f32[1,16,256]{2,1,0:T(8,128)S(1)}, f32[1,16,256]{2,1,0:T(8,128)}, u32[]{:S(2)}) copy-start(f32[1,16,256]{2,1,0:T(8,128)} %param.14) | copy-start | bytes 49156
Sparse Core Ops, SparseCore 0:
  230.2 168.7 reduce-scatter.1
where the time goes:
time: 408 us
  waiting for transfers between devices  169 us (41%)
  blocking collectives  88.2 us (22%)
  local copies, waits for them, and re-layouts  83.9 us (21%)
  matrix products  43.7 us (11%)
  between operations  13.6 us (3%)
  other arithmetic  5.66 us (1%)
    reduce_scatter x1, waiting for transfers between devices, per_device(): lax.psum_scatter(lax.dot_general(out_weight, gated_rows, (((0,), (1,)), (...  169 us
    all_gather x2, blocking collectives, prefix(): pieces = jax.tree.map(lambda part: lax.all_gather(part, axis), value)  88.2 us
    gather x2, local copies, waits for them, and re-layouts, per_device(): kernel[jnp.maximum(offset, 0)]  80.2 us
    dot_general x1, matrix products, per_device(): within = jnp.einsum('tjc,sbjc->sbtc', toeplitz, blocked, precision=highest)  28.6 us
    dot_general x1, matrix products, per_device(): lax.dot_general(out_weight, gated_rows, (((0,), (1,)), ((), ())), preferr...  8.52 us
  transfers between devices with their start and end apart: 2, of which 1 were waited for; matrix products, arithmetic and copies ran while one was open for 21% of the time, Pallas kernels for 0%

commit v1 on v0

v1 whole, which is shorter than its diff:
```python
import jax
import jax.numpy as jnp
from jax import lax
from jax.experimental import pallas as pl
from jax.experimental.pallas import tpu as pltpu
from jax.sharding import PartitionSpec as P

MESH = pl.DeviceIdType.MESH
F32 = jnp.float32
BF16 = jnp.bfloat16

NX, NZ, NY, NH = 4, 4, 4, 2
SUB = 8
LANES = 128
HALO = 16


def order_of(z, k):
    if k == 0:
        return jnp.where(z < 2, 3, 0)
    if k == 1:
        return jnp.where(z == 0, 2, jnp.where(z == 1, 0, jnp.where(z == 2, 3, 1)))
    if k == 2:
        return jnp.where(z % 2 == 0, 1, 2)
    return z


def kernel(
    streams, taps, decay, residues, init, weight, out,
    xbf, halo, xs, q_s, d_s, r_s, tapb, decb, resb, lst, ent, ebuf, tbuf, own_e,
    w_own, w_far, gat, pbuf, sendbuf, rbuf, pfin,
    load_sem, wload_sem, halo_sem, e_ssem, e_rsem, t_sem,
    wp_ssem, wp_rsem, wd_ssem, wd_rsem, f1_ssem, f1_rsem, f2_ssem, f2_rsem,
    g_ssem, g_rsem, gp_ssem, gp_rsem, z_ssem, z_rsem,
):
    tp, ctx = lax.axis_index("tp"), lax.axis_index("ctx")
    core, x, z = tp % 2, (tp // 2) % NX, tp // (2 * NX)
    y, zh = ctx % NY, ctx // NY
    nctx = NY * NH
    length = streams.shape[2]
    chans = streams.shape[3]
    poles = decay.shape[0]
    tap_count = taps.shape[1]
    lag = tap_count - 1
    sub_len = length // SUB
    half = length // 2
    groups = chans // LANES
    quarter = chans // NY

    def tp_of(zi, xi, ci):
        return (zi * NX + xi) * 2 + ci

    def dev(tp_index=tp, ctx_index=ctx):
        return {"ctx": ctx_index, "tp": tp_index}

    def remote(src, dst, ssem, rsem, where):
        return pltpu.make_async_remote_copy(
            src_ref=src, dst_ref=dst, send_sem=ssem, recv_sem=rsem, device_id=where, device_id_type=MESH
        )

    def ctx_of(hi, yi):
        return hi * NY + yi

    partner = dev(tp_of(z, x, 1 - core))
    xp, xm = (x + 1) % NX, (x + NX - 1) % NX
    yp, ym = (y + 1) % NY, (y + NY - 1) % NY
    ctx_next, ctx_prev = (ctx + 1) % nctx, (ctx + nctx - 1) % nctx

    barrier = pltpu.get_barrier_semaphore()
    greeted = [partner, dev(tp_of((z + 1) % NZ, x, core)), dev(tp_of((z + NZ - 1) % NZ, x, core))]
    for dx in range(1, NX):
        for dc in range(2):
            greeted.append(dev(tp_of(z, (x + dx) % NX, (core + dc) % 2)))
    for dy in range(1, NY):
        greeted.append(dev(tp, ctx_of(zh, (y + dy) % NY)))
    greeted += [dev(tp, ctx_next), dev(tp, ctx_prev), dev(tp, ctx_of(1 - zh, y))]
    for where in greeted:
        pl.semaphore_signal(barrier, inc=1, device_id=where, device_id_type=MESH)

    load = pltpu.make_async_copy(streams.at[:, 0], xbf, load_sem)
    load.start()

    def w_cols(zt, xi, ci):
        return pl.ds(pl.multiple_of(tp_of(zt, xi, ci) * chans, chans), chans)

    own_loads = []
    for k in range(NZ):
        zt = order_of(z, k)
        own_loads.append(
            pltpu.make_async_copy(weight.at[:, w_cols(zt, x, core)], w_own.at[k, pl.ds(0, chans)], wload_sem.at[k])
        )
    load.wait()

    for g in range(groups):
        lanes = slice(g * LANES, (g + 1) * LANES)
        for s in range(3):
            for i in range(tap_count):
                tapb[g, s * tap_count + i] = jnp.broadcast_to(taps[s, i : i + 1, lanes], (SUB, LANES))
        for n in range(poles):
            decb[g, n] = jnp.broadcast_to(decay[n : n + 1, lanes], (SUB, LANES))
            resb[g, n] = jnp.broadcast_to(residues[n : n + 1, lanes], (SUB, LANES))
        for s in range(3):
            xs[s * groups + g, pl.ds(HALO, length), :] = xbf[s, :, lanes].astype(F32)

    def featurize(first, last):
        for g in range(groups):
            def one(j, carry, g=g):
                feats = []
                for s in range(3):
                    total = None
                    for i in range(tap_count):
                        rows = xs[s * groups + g, pl.ds(HALO + j - i, SUB, stride=sub_len), :]
                        term = tapb[g, s * tap_count + i] * rows
                        total = term if total is None else total + term
                    feats.append(total)
                q_s[g, j] = feats[0]
                d_s[g, j] = feats[1] * feats[2]
                return carry

            lax.fori_loop(first, last, one, 0, unroll=2)

    featurize(lag, sub_len)

    pl.semaphore_wait(barrier, len(greeted))

    halo_copy = remote(
        streams.at[:, 0, pl.ds(length - HALO, HALO)], halo, halo_sem.at[0], halo_sem.at[1], dev(tp, ctx_next)
    )

    @pl.when(ctx < nctx - 1)
    def _():
        halo_copy.start()

    wp_copies, wd_copies = [], []
    for k in range(NZ):
        zt = order_of(z, k)
        own_loads[k].start()
        copy = remote(
            weight.at[:, w_cols(zt, x, 1 - core)], w_own.at[k, pl.ds(chans, chans)], wp_ssem.at[k], wp_rsem.at[k], partner
        )
        copy.start()
        wp_copies.append(copy)
        rows = pl.ds(pl.multiple_of(y * quarter, quarter), quarter)
        sends = []
        for dx in (1, 3, 2):
            for dc in range(2):
                xi, ci = (x + dx) % NX, (core + dc) % 2
                slot = (NX - dx) * 2 + dc - 2
                copy = remote(
                    weight.at[rows, w_cols(zt, xi, ci)],
                    w_far.at[k, y, pl.ds(slot * quarter, quarter)],
                    wd_ssem.at[k, slot], wd_rsem.at[k, slot], dev(tp_of(z, xi, ci)),
                )
                copy.start()
                sends.append(copy)
        wd_copies.append(sends)

    far_rows = w_far.shape[2]
    y_next, y_prev = dev(tp, ctx_of(zh, yp)), dev(tp, ctx_of(zh, ym))
    y_opp = (y + 2) % NY
    f1 = [
        [
            remote(w_far.at[k, y], w_far.at[k, y], f1_ssem.at[k, d], f1_rsem.at[k, d], where)
            for d, where in enumerate((y_next, y_prev))
        ]
        for k in range(NZ)
    ]
    top, bottom = pl.ds(0, far_rows // 2), pl.ds(far_rows // 2, far_rows // 2)
    f2 = [
        [
            remote(w_far.at[k, ym, top], w_far.at[k, ym, top], f2_ssem.at[k, 0], f2_rsem.at[k, 0], y_next),
            remote(w_far.at[k, yp, bottom], w_far.at[k, yp, bottom], f2_ssem.at[k, 1], f2_rsem.at[k, 1], y_prev),
        ]
        for k in range(NZ)
    ]

    def forward_once(k):
        for copy in wd_copies[k]:
            copy.wait_recv()
        for copy in f1[k]:
            copy.start()

    def forward_twice(k):
        for copy in f1[k]:
            copy.wait_recv()
        for copy in f2[k]:
            copy.start()

    @pl.when(ctx > 0)
    def _():
        halo_copy.wait_recv()
        for g in range(groups):
            for s in range(3):
                xs[s * groups + g, pl.ds(0, HALO), :] = halo[s, :, g * LANES : (g + 1) * LANES].astype(F32)

    @pl.when(ctx == 0)
    def _():
        for g in range(groups):
            for s in range(3):
                xs[s * groups + g, pl.ds(0, HALO), :] = jnp.zeros((HALO, LANES), F32)

    featurize(0, lag)

    for g in range(groups):
        def step(j, states, g=g):
            driven = d_s[g, j]
            new = tuple(decb[g, n] * states[n] + driven for n in range(poles))
            parts = [resb[g, n] * new[n] for n in range(poles)]
            while len(parts) > 1:
                parts = [a + b for a, b in zip(parts[::2], parts[1::2])]
            r_s[g, j] = parts[0]
            return new

        states = lax.fori_loop(0, sub_len, step, tuple(jnp.zeros((SUB, LANES), F32) for _ in range(poles)), unroll=2)
        for n in range(poles):
            lst[g, pl.ds(n * SUB, SUB), :] = states[n]

    def power(value, count):
        result, base = None, value
        while count:
            if count % 2:
                result = base if result is None else result * base
            count //= 2
            if count:
                base = base * base
        return result

    for g in range(groups):
        lanes = slice(g * LANES, (g + 1) * LANES)
        sub_decay = power(decay[:, lanes], sub_len)
        running = jnp.zeros((poles, LANES), F32)
        for s in range(SUB):
            ent[g, s] = running
            running = sub_decay * running + lst[g, pl.ds(s, poles, stride=SUB), :]
        own_e[:, lanes] = running

    e_copies = [
        remote(own_e, ebuf.at[dy - 1], e_ssem.at[dy - 1], e_rsem.at[dy - 1], dev(tp, ctx_of(zh, (y + dy) % NY)))
        for dy in range(1, NY)
    ]
    for copy in e_copies:
        copy.start()

    forward_once(0)

    for copy in e_copies:
        copy.wait_recv()

    def select_power(powers, exponent):
        value = jnp.broadcast_to(jnp.where(exponent == 0, F32(1.0), F32(0.0)), powers[0].shape)
        for e, p in enumerate(powers):
            value = jnp.where(exponent == e + 1, p, value)
        return value

    t_copy = remote(tbuf.at[0], tbuf.at[1], t_sem.at[0], t_sem.at[1], dev(tp, ctx_of(1 - zh, y)))

    shard_decay = power(decay[...], length)
    powers = [shard_decay, shard_decay * shard_decay]
    powers.append(powers[1] * shard_decay)

    @pl.when(zh == 0)
    def _():
        total = powers[2] * shard_decay * init[0] + select_power(powers, 3 - y) * own_e[...]
        for dy in range(1, NY):
            total = total + select_power(powers, 3 - (y + NY - dy) % NY) * ebuf[dy - 1]
        tbuf[0] = total
        t_copy.start()
        tbuf[2] = init[0]

    @pl.when(zh == 1)
    def _():
        t_copy.wait_recv()
        tbuf[2] = tbuf[1]

    incoming = select_power(powers, y) * tbuf[2]
    for dy in range(1, NY):
        gain = F32(1.0) if dy == 1 else powers[dy - 2]
        incoming = incoming + jnp.where(y >= dy, gain * ebuf[dy - 1], F32(0.0))

    for g in range(groups):
        lanes = slice(g * LANES, (g + 1) * LANES)
        sub_decay = power(decay[:, lanes], sub_len)
        arriving = incoming[:, lanes]
        for s in range(SUB):
            lst[g, pl.ds(s, poles, stride=SUB), :] = (ent[g, s] + arriving) * residues[:, lanes]
            arriving = arriving * sub_decay

    for g in range(groups):
        states = tuple(lst[g, pl.ds(n * SUB, SUB), :] for n in range(poles))
        for h in range(2):
            def pair(jj, states, g=g, h=h):
                rows = []
                for b in range(2):
                    j = h * (sub_len // 2) + 2 * jj + b
                    states = tuple(decb[g, n] * states[n] for n in range(poles))
                    parts = list(states)
                    while len(parts) > 1:
                        parts = [u + v for u, v in zip(parts[::2], parts[1::2])]
                    rows.append(q_s[g, j] * (r_s[g, j] + parts[0]))
                at = pl.ds(pl.multiple_of(jj * 2 * SUB, 2 * SUB), 2 * SUB)
                gat[h, at, g * LANES : (g + 1) * LANES] = jnp.concatenate(rows, axis=0).astype(BF16)
                return states

            states = lax.fori_loop(0, sub_len // 4, pair, states)

    def block(h, slot):
        return gat.at[h, :, pl.ds(slot * chans, chans)]

    def g_copy(h, src_slot, dst_slot, at, where):
        return remote(block(h, src_slot), block(h, dst_slot), g_ssem.at[at], g_rsem.at[at], where)

    def p_copy(h, slot):
        return remote(
            block(h, slot), block(h, slot + 1), gp_ssem.at[h, slot // 2], gp_rsem.at[h, slot // 2], partner
        )

    to_right, to_left = dev(tp_of(z, xp, core)), dev(tp_of(z, xm, core))
    right = [g_copy(0, 0, 6, 0, to_right), g_copy(1, 0, 6, 1, to_right)]
    left = [g_copy(0, 0, 2, 2, to_left), g_copy(1, 0, 2, 3, to_left)]
    relay_right = g_copy(0, 6, 4, 4, to_right)
    relay_left = g_copy(1, 2, 4, 5, to_left)
    right[0].start()
    left[1].start()
    right[1].start()
    left[0].start()
    p_copies = [[p_copy(h, slot) for slot in (0, 2, 4, 6)] for h in range(2)]
    for h in range(2):
        p_copies[h][0].start()

    forward_once(1)
    right[0].wait_recv()
    relay_right.start()
    p_copies[0][3].start()
    left[1].wait_recv()
    relay_left.start()
    p_copies[1][1].start()
    right[1].wait_recv()
    p_copies[1][3].start()
    left[0].wait_recv()
    p_copies[0][1].start()
    forward_twice(0)
    forward_once(2)
    relay_right.wait_recv()
    p_copies[0][2].start()
    relay_left.wait_recv()
    p_copies[1][2].start()
    forward_twice(1)
    for h in range(2):
        for copy in p_copies[h]:
            copy.wait_recv()

    z_copies = []
    for k in range(NZ):
        if k == 1:
            forward_once(3)
            forward_twice(2)
        if k == 2:
            forward_twice(3)
        zt = order_of(z, k)
        own_loads[k].wait()
        wp_copies[k].wait_recv()
        for copy in f2[k]:
            copy.wait_recv()
        pieces = [w_own[k]]
        for slot in range(2 * NX - 2):
            for q in range(NY):
                pieces.append(w_far[k, q, slot * quarter : (slot + 1) * quarter])
        w_all = jnp.concatenate(pieces, axis=0)
        for h in range(2):
            product = jnp.dot(gat[h], w_all, preferred_element_type=F32)
            if k < NZ - 1:
                heading = jnp.where(zt > z, 0, 1)
                target = jnp.where(zt > z, z + 1, z - 1)
                copy = remote(
                    sendbuf.at[k, h], rbuf.at[heading, zt, h], z_ssem.at[k, h], z_rsem.at[heading, zt, h],
                    dev(tp_of(target, x, core)),
                )
                pbuf[...] = product
                has_in = jnp.where(zt > z, z > 0, z < NZ - 1)

                @pl.when(has_in)
                def _(copy=copy, heading=heading, zt=zt, h=h):
                    copy.wait_recv()
                    pbuf[...] += rbuf[heading, zt, h].astype(F32)

                sendbuf[k, h] = pbuf[...].astype(BF16)
                copy.start()
                z_copies.append(copy)
            else:
                pbuf[...] = product

                @pl.when(z > 0)
                def _(h=h):
                    remote(
                        sendbuf.at[0, h], rbuf.at[0, z, h], z_ssem.at[0, h], z_rsem.at[0, z, h], partner
                    ).wait_recv()
                    pbuf[...] += rbuf[0, z, h].astype(F32)

                @pl.when(z < NZ - 1)
                def _(h=h):
                    remote(
                        sendbuf.at[0, h], rbuf.at[1, z, h], z_ssem.at[0, h], z_rsem.at[1, z, h], partner
                    ).wait_recv()
                    pbuf[...] += rbuf[1, z, h].astype(F32)

                for g in range(groups):
                    pfin[g, pl.ds(h * half, half), :] = pbuf[:, g * LANES : (g + 1) * LANES]

    for g in range(groups):
        for s in range(SUB):
            out[0, s * sub_len : (s + 1) * sub_len, g * LANES : (g + 1) * LANES] = pfin[
                g, pl.ds(s, sub_len, stride=SUB), :
            ].astype(BF16)

    @pl.when(ctx < nctx - 1)
    def _():
        halo_copy.wait_send()

    @pl.when(zh == 0)
    def _():
        t_copy.wait_send()

    sent = e_copies + wp_copies + right + left + [relay_right, relay_left] + z_copies
    for k in range(NZ):
        sent = sent + wd_copies[k] + f1[k] + f2[k]
    for h in range(2):
        sent = sent + p_copies[h]
    for copy in sent:
        copy.wait_send()


def per_device(streams, taps, decay, residues, init_state, out_weight):
    length, chans = streams.shape[2], streams.shape[3]
    poles, tap_count = decay.shape[0], taps.shape[1]
    groups, sub_len, half, quarter = chans // LANES, length // SUB, length // 2, chans // NY
    vmem = pl.BlockSpec(memory_space=pltpu.VMEM)
    hbm = pl.BlockSpec(memory_space=pl.ANY)
    dma = pltpu.SemaphoreType.DMA
    return pl.pallas_call(
        kernel,
        out_shape=jax.ShapeDtypeStruct((1, length, chans), BF16),
        in_specs=[hbm, vmem, vmem, vmem, vmem, hbm],
        out_specs=vmem,
        scratch_shapes=[
            pltpu.VMEM((3, length, chans), BF16),
            pltpu.VMEM((3, HALO, chans), BF16),
            pltpu.VMEM((3 * groups, HALO + length, LANES), F32),
            pltpu.VMEM((groups, sub_len, SUB, LANES), F32),
            pltpu.VMEM((groups, sub_len, SUB, LANES), F32),
            pltpu.VMEM((groups, sub_len, SUB, LANES), F32),
            pltpu.VMEM((groups, 3 * tap_count, SUB, LANES), F32),
            pltpu.VMEM((groups, poles, SUB, LANES), F32),
            pltpu.VMEM((groups, poles, SUB, LANES), F32),
            pltpu.VMEM((groups, poles * SUB, LANES), F32),
            pltpu.VMEM((groups, SUB, poles, LANES), F32),
            pltpu.VMEM((NY - 1, poles, chans), F32),
            pltpu.VMEM((3, poles, chans), F32),
            pltpu.VMEM((poles, chans), F32),
            pltpu.VMEM((NZ, 2 * chans, chans), BF16),
            pltpu.VMEM((NZ, NY, (2 * NX - 2) * quarter, chans), BF16),
            pltpu.VMEM((2, half, 2 * NX * chans), BF16),
            pltpu.VMEM((half, chans), F32),
            pltpu.VMEM((NZ - 1, 2, half, chans), BF16),
            pltpu.VMEM((2, NZ, 2, half, chans), BF16),
            pltpu.VMEM((groups, length, LANES), F32),
            dma(()), dma((NZ,)), dma((2,)), dma((NY - 1,)), dma((NY - 1,)), dma((2,)),
            dma((NZ,)), dma((NZ,)), dma((NZ, 2 * NX - 2)), dma((NZ, 2 * NX - 2)),
            dma((NZ, 2)), dma((NZ, 2)), dma((NZ, 2)), dma((NZ, 2)),
            dma((6,)), dma((6,)), dma((2, NX)), dma((2, NX)),
            dma((NZ - 1, 2)), dma((2, NZ, 2)),
        ],
        compiler_params=pltpu.CompilerParams(
            collective_id=0, has_side_effects=True, vmem_limit_bytes=62 * 1024 * 1024
        ),
        name="hyena_li",
    )(streams, taps, decay, residues, init_state, out_weight)


def solution(mesh):
    in_specs = (
        P(None, None, "ctx", "tp"),
        P(None, None, "tp"),
        P(None, "tp"),
        P(None, "tp"),
        P(None, None, "tp"),
        P("tp", None),
    )
    return jax.shard_map(
        per_device, mesh=mesh, in_specs=in_specs, out_specs=P(None, "ctx", "tp"), check_vma=False
    )
```

time: 408 us -> 57.7 us (0.14)
  the two profiles are of different devices: /device:TPU:16 before, /device:TPU:32 now
where the time goes in v1:
time: 57.7 us; the launch traced here: 57.5 us
  Pallas kernels  55.9 us (97%)
  local copies, waits for them, and re-layouts  1.62 us (3%)
    pallas_call x1, Pallas kernels, per_device(): pl.pallas_call(kernel, out_shape=jax.ShapeDtypeStruct((1, length, chans),...  55.9 us
    unnamed x1, local copies, waits for them, and re-layouts  1.62 us

profile of v1, /device:TPU:32, one launch (start us, length us, event | category | flops | bytes accessed | tf_op | source)
XLA Modules:
  0.0 57.5 jit_solution(7286813189588055583)
XLA Ops:
  0.0 55.9 %hyena_li.1 = bf16[1,384,256]{2,1,0:T(8,128)(2,1)} custom-call(bf16[3,1,384,256]{3,2,1,0:T(8,128)(2,1)} %streams.1, f32[3,7,256]{2,1,0:T(8,128)} %taps.1, f32[16,256]{1,0:T(8,128)} %decay.1, f32[16,256]{1,0:T(8,128)} %residues.1, f32[1,16,256]{2,1,0:T(8,128)} %init.1, bf16[256,8192]{1,0:T(8,128)(2,1)} %weight.1), custom_call_target="tpu_custom_call" | custom-call | tf_op jit(solution)/shard_map/hyena_li/pallas_call | solution.py:439
  55.9 1.6 %copy.8 = bf16[1,384,256]{2,1,0:T(8,128)(2,1)} copy(bf16[1,384,256]{2,1,0:T(8,128)(2,1)} %hyena_li.1) | data formatting | bytes 393216

commit v2 on v1

--- a/solution.py
+++ b/solution.py
@@ -8,6 +8,20 @@
 MESH = pl.DeviceIdType.MESH
 F32 = jnp.float32
 BF16 = jnp.bfloat16
+BY_X = (2, 3)
+
+PLAN = {
+    'barrier': ('p0', 'd0', 'd1', 'p1', 'p2', 'p3'),
+    'states': (),
+    'sent': ('d2', 'd3', 'f0'),
+    'ends': (),
+    'total': ('f1',),
+    'gated': ('r0',),
+    'near': ('l2',),
+    'far': ('f2', 'r1', 'l3'),
+    'k1': ('f3',),
+    'k2': (),
+}
 
 NX, NZ, NY, NH = 4, 4, 4, 2
 SUB = 8
@@ -30,7 +44,7 @@
     xbf, halo, xs, q_s, d_s, r_s, tapb, decb, resb, lst, ent, ebuf, tbuf, own_e,
     w_own, w_far, gat, pbuf, sendbuf, rbuf, pfin,
     load_sem, wload_sem, halo_sem, e_ssem, e_rsem, t_sem,
-    wp_ssem, wp_rsem, wd_ssem, wd_rsem, f1_ssem, f1_rsem, f2_ssem, f2_rsem,
+    wp_ssem, wp_rsem, wd_ssem, wd_rsem, ready_sem, f1_ssem, f1_rsem, f2_ssem, f2_rsem,
     g_ssem, g_rsem, gp_ssem, gp_rsem, z_ssem, z_rsem,
 ):
     tp, ctx = lax.axis_index("tp"), lax.axis_index("ctx")
@@ -67,15 +81,45 @@
     ctx_next, ctx_prev = (ctx + 1) % nctx, (ctx + nctx - 1) % nctx
 
     barrier = pltpu.get_barrier_semaphore()
-    greeted = [partner, dev(tp_of((z + 1) % NZ, x, core)), dev(tp_of((z + NZ - 1) % NZ, x, core))]
+
+    def signal(where, sem=barrier):
+        pl.semaphore_signal(sem, inc=1, device_id=where, device_id_type=MESH)
+
+    greeted = [partner]
     for dx in range(1, NX):
         for dc in range(2):
             greeted.append(dev(tp_of(z, (x + dx) % NX, (core + dc) % 2)))
     for dy in range(1, NY):
         greeted.append(dev(tp, ctx_of(zh, (y + dy) % NY)))
-    greeted += [dev(tp, ctx_next), dev(tp, ctx_prev), dev(tp, ctx_of(1 - zh, y))]
+    last_low = jnp.logical_and(zh == 0, y == NY - 1)
+    first_high = jnp.logical_and(zh == 1, y == 0)
+
+    @pl.when(first_high)
+    def _():
+        signal(dev(tp, ctx_prev))
+
     for where in greeted:
-        pl.semaphore_signal(barrier, inc=1, device_id=where, device_id_type=MESH)
+        signal(where)
+
+    @pl.when(z > 0)
+    def _():
+        signal(dev(tp_of(z - 1, x, core)))
+
+    @pl.when(z < NZ - 1)
+    def _():
+        signal(dev(tp_of(z + 1, x, core)))
+
+    inner = jnp.where(z == 0, 1, jnp.where(z == NZ - 1, 1, 2))
+    across = dev(tp, ctx_of(1 - zh, y))
+    sent, awaited = [], []
+
+    def go(copy):
+        copy.start()
+        sent.append(copy)
+
+    def got(copy):
+        copy.wait_recv()
+        awaited.append(copy)
 
     load = pltpu.make_async_copy(streams.at[:, 0], xbf, load_sem)
     load.start()
@@ -121,7 +165,20 @@
 
     featurize(lag, sub_len)
 
-    pl.semaphore_wait(barrier, len(greeted))
+    pl.semaphore_wait(barrier, len(greeted) + inner + jnp.where(last_low, 1, jnp.where(first_high, 2, zh)))
+
+    @pl.when(zh == 0)
+    def _():
+        signal(across)
+
+    @pl.when(last_low)
+    def _():
+        signal(dev(tp, ctx_next))
+
+    @pl.when(zh == 1)
+    def _():
+        signal(across, ready_sem)
+
 
     halo_copy = remote(
         streams.at[:, 0, pl.ds(length - HALO, HALO)], halo, halo_sem.at[0], halo_sem.at[1], dev(tp, ctx_next)
@@ -131,33 +188,38 @@
     def _():
         halo_copy.start()
 
-    wp_copies, wd_copies = [], []
-    for k in range(NZ):
-        zt = order_of(z, k)
+    wp_copies = [
+        remote(
+            weight.at[:, w_cols(order_of(z, k), x, 1 - core)],
+            w_own.at[k, pl.ds(chans, chans)], wp_ssem.at[k], wp_rsem.at[k], partner,
+        )
+        for k in range(NZ)
+    ]
+
+    def own_rows(k):
         own_loads[k].start()
-        copy = remote(
-            weight.at[:, w_cols(zt, x, 1 - core)], w_own.at[k, pl.ds(chans, chans)], wp_ssem.at[k], wp_rsem.at[k], partner
-        )
-        copy.start()
-        wp_copies.append(copy)
-        rows = pl.ds(pl.multiple_of(y * quarter, quarter), quarter)
+        go(wp_copies[k])
+
+    def direct(k, q, kind):
+        rows = pl.ds(pl.multiple_of(q * quarter, quarter), quarter)
         sends = []
         for dx in (1, 3, 2):
             for dc in range(2):
                 xi, ci = (x + dx) % NX, (core + dc) % 2
                 slot = (NX - dx) * 2 + dc - 2
                 copy = remote(
-                    weight.at[rows, w_cols(zt, xi, ci)],
-                    w_far.at[k, y, pl.ds(slot * quarter, quarter)],
-                    wd_ssem.at[k, slot], wd_rsem.at[k, slot], dev(tp_of(z, xi, ci)),
+                    weight.at[rows, w_cols(order_of(z, k), xi, ci)],
+                    w_far.at[k, q, pl.ds(slot * quarter, quarter)],
+                    wd_ssem.at[kind, k, slot], wd_rsem.at[kind, k, slot], dev(tp_of(z, xi, ci)),
                 )
-                copy.start()
                 sends.append(copy)
-        wd_copies.append(sends)
+        return sends
+
+    wd_copies = [direct(k, y, 0) for k in range(NZ)]
+    late = {k: direct(k, (y + 2) % NY, 1) for k in BY_X}
 
     far_rows = w_far.shape[2]
     y_next, y_prev = dev(tp, ctx_of(zh, yp)), dev(tp, ctx_of(zh, ym))
-    y_opp = (y + 2) % NY
     f1 = [
         [
             remote(w_far.at[k, y], w_far.at[k, y], f1_ssem.at[k, d], f1_rsem.at[k, d], where)
@@ -167,24 +229,40 @@
     ]
     top, bottom = pl.ds(0, far_rows // 2), pl.ds(far_rows // 2, far_rows // 2)
     f2 = [
-        [
+        []
+        if k in BY_X
+        else [
             remote(w_far.at[k, ym, top], w_far.at[k, ym, top], f2_ssem.at[k, 0], f2_rsem.at[k, 0], y_next),
             remote(w_far.at[k, yp, bottom], w_far.at[k, yp, bottom], f2_ssem.at[k, 1], f2_rsem.at[k, 1], y_prev),
         ]
         for k in range(NZ)
     ]
 
-    def forward_once(k):
-        for copy in wd_copies[k]:
-            copy.wait_recv()
-        for copy in f1[k]:
-            copy.start()
-
-    def forward_twice(k):
-        for copy in f1[k]:
-            copy.wait_recv()
-        for copy in f2[k]:
-            copy.start()
+    def act(kind, k):
+        if kind == "p":
+            own_rows(k)
+        if kind == "d":
+            for copy in wd_copies[k]:
+                go(copy)
+        if kind == "l":
+            for copy in late[k]:
+                go(copy)
+        if kind == "f":
+            for copy in wd_copies[k]:
+                got(copy)
+            for copy in f1[k]:
+                go(copy)
+        if kind == "r":
+            for copy in f1[k]:
+                got(copy)
+            for copy in f2[k]:
+                go(copy)
+
+    def point(name):
+        for step in PLAN[name]:
+            act(step[0], int(step[1]))
+
+    point("barrier")
 
     @pl.when(ctx > 0)
     def _():
@@ -200,6 +278,8 @@
                 xs[s * groups + g, pl.ds(0, HALO), :] = jnp.zeros((HALO, LANES), F32)
 
     featurize(0, lag)
+
+    point("states")
 
     for g in range(groups):
         def step(j, states, g=g):
@@ -239,12 +319,14 @@
         for dy in range(1, NY)
     ]
     for copy in e_copies:
-        copy.start()
-
-    forward_once(0)
+        go(copy)
+
+    point("sent")
 
     for copy in e_copies:
-        copy.wait_recv()
+        got(copy)
+
+    point("ends")
 
     def select_power(powers, exponent):
         value = jnp.broadcast_to(jnp.where(exponent == 0, F32(1.0), F32(0.0)), powers[0].shape)
@@ -264,6 +346,7 @@
         for dy in range(1, NY):
             total = total + select_power(powers, 3 - (y + NY - dy) % NY) * ebuf[dy - 1]
         tbuf[0] = total
+        pl.semaphore_wait(ready_sem, 1)
         t_copy.start()
         tbuf[2] = init[0]
 
@@ -276,6 +359,8 @@
     for dy in range(1, NY):
         gain = F32(1.0) if dy == 1 else powers[dy - 2]
         incoming = incoming + jnp.where(y >= dy, gain * ebuf[dy - 1], F32(0.0))
+
+    point("total")
 
     for g in range(groups):
         lanes = slice(g * LANES, (g + 1) * LANES)
@@ -319,48 +404,46 @@
     left = [g_copy(0, 0, 2, 2, to_left), g_copy(1, 0, 2, 3, to_left)]
     relay_right = g_copy(0, 6, 4, 4, to_right)
     relay_left = g_copy(1, 2, 4, 5, to_left)
-    right[0].start()
-    left[1].start()
-    right[1].start()
-    left[0].start()
+    go(right[0])
+    go(left[1])
+    go(right[1])
+    go(left[0])
     p_copies = [[p_copy(h, slot) for slot in (0, 2, 4, 6)] for h in range(2)]
     for h in range(2):
-        p_copies[h][0].start()
-
-    forward_once(1)
-    right[0].wait_recv()
-    relay_right.start()
-    p_copies[0][3].start()
-    left[1].wait_recv()
-    relay_left.start()
-    p_copies[1][1].start()
-    right[1].wait_recv()
-    p_copies[1][3].start()
-    left[0].wait_recv()
-    p_copies[0][1].start()
-    forward_twice(0)
-    forward_once(2)
-    relay_right.wait_recv()
-    p_copies[0][2].start()
-    relay_left.wait_recv()
-    p_copies[1][2].start()
-    forward_twice(1)
+        go(p_copies[h][0])
+
+    point("gated")
+    got(right[0])
+    go(relay_right)
+    go(p_copies[0][3])
+    got(left[1])
+    go(relay_left)
+    go(p_copies[1][1])
+    got(right[1])
+    go(p_copies[1][3])
+    got(left[0])
+    go(p_copies[0][1])
+    point("near")
+    got(relay_right)
+    go(p_copies[0][2])
+    got(relay_left)
+    go(p_copies[1][2])
+    point("far")
     for h in range(2):
         for copy in p_copies[h]:
-            copy.wait_recv()
-
-    z_copies = []
+            got(copy)
+
     for k in range(NZ):
-        if k == 1:
-            forward_once(3)
-            forward_twice(2)
-        if k == 2:
-            forward_twice(3)
+        if k in (1, 2):
+            point("k1" if k == 1 else "k2")
         zt = order_of(z, k)
         own_loads[k].wait()
-        wp_copies[k].wait_recv()
+        got(wp_copies[k])
+        if k in BY_X:
+            for copy in f1[k] + late[k]:
+                got(copy)
         for copy in f2[k]:
-            copy.wait_recv()
+            got(copy)
         pieces = [w_own[k]]
         for slot in range(2 * NX - 2):
             for q in range(NY):
@@ -380,12 +463,11 @@
 
                 @pl.when(has_in)
                 def _(copy=copy, heading=heading, zt=zt, h=h):
-                    copy.wait_recv()
+                    got(copy)
                     pbuf[...] += rbuf[heading, zt, h].astype(F32)
 
                 sendbuf[k, h] = pbuf[...].astype(BF16)
-                copy.start()
-                z_copies.append(copy)
+                go(copy)
             else:
                 pbuf[...] = product
 
@@ -420,11 +502,6 @@
     def _():
         t_copy.wait_send()
 
-    sent = e_copies + wp_copies + right + left + [relay_right, relay_left] + z_copies
-    for k in range(NZ):
-        sent = sent + wd_copies[k] + f1[k] + f2[k]
-    for h in range(2):
-        sent = sent + p_copies[h]
     for copy in sent:
         copy.wait_send()
 
@@ -464,7 +541,7 @@
             pltpu.VMEM((2, NZ, 2, half, chans), BF16),
             pltpu.VMEM((groups, length, LANES), F32),
             dma(()), dma((NZ,)), dma((2,)), dma((NY - 1,)), dma((NY - 1,)), dma((2,)),
-            dma((NZ,)), dma((NZ,)), dma((NZ, 2 * NX - 2)), dma((NZ, 2 * NX - 2)),
+            dma((NZ,)), dma((NZ,)), dma((2, NZ, 2 * NX - 2)), dma((2, NZ, 2 * NX - 2)), pltpu.SemaphoreType.REGULAR,
             dma((NZ, 2)), dma((NZ, 2)), dma((NZ, 2)), dma((NZ, 2)),
             dma((6,)), dma((6,)), dma((2, NX)), dma((2, NX)),
             dma((NZ - 1, 2)), dma((2, NZ, 2)),

time: 57.7 us -> 52.7 us (0.913)
  Pallas kernels: 55.9 us -> 50.3 us
    pallas_call x1, Pallas kernels: 55.9 us -> 50.3 us  [per_device(): pl.pallas_call(kernel, out_shape=jax.ShapeDtypeStruct((1, length, chans),...]
where the time goes in v2:
time: 52.7 us; the launch traced here: 51.9 us
  Pallas kernels  50.3 us (95%)
  local copies, waits for them, and re-layouts  1.62 us (3%)
    pallas_call x1, Pallas kernels, per_device(): pl.pallas_call(kernel, out_shape=jax.ShapeDtypeStruct((1, length, chans),...  50.3 us
    unnamed x1, local copies, waits for them, and re-layouts  1.62 us

profile of v2, /device:TPU:32, one launch (start us, length us, event | category | flops | bytes accessed | tf_op | source)
XLA Modules:
  0.0 51.9 jit_solution(9304477022475646446)
XLA Ops:
  0.0 50.3 %hyena_li.1 = bf16[1,384,256]{2,1,0:T(8,128)(2,1)} custom-call(bf16[3,1,384,256]{3,2,1,0:T(8,128)(2,1)} %streams.1, f32[3,7,256]{2,1,0:T(8,128)} %taps.1, f32[16,256]{1,0:T(8,128)} %decay.1, f32[16,256]{1,0:T(8,128)} %residues.1, f32[1,16,256]{2,1,0:T(8,128)} %init.1, bf16[256,8192]{1,0:T(8,128)(2,1)} %weight.1), custom_call_target="tpu_custom_call" | custom-call | tf_op jit(solution)/shard_map/hyena_li/pallas_call | solution.py:516
  50.3 1.6 %copy.8 = bf16[1,384,256]{2,1,0:T(8,128)(2,1)} copy(bf16[1,384,256]{2,1,0:T(8,128)(2,1)} %hyena_li.1) | data formatting | bytes 393216
